TPU v7x, 128 devices: a whole 4x4x4 slice. The times are simulated.
128 devices in a mesh: lev: 8 (over x, z_lo), mem: 16 (over z_hi, y, core).
Axes of the slice: x: 4, y: 4, z: 4 (z_hi: 2, z_lo: 2; z = z_hi * 2 + z_lo), core: 2. Of those that a mesh axis runs over, the one named last changes fastest.
Arguments:
- control: float32 [4096, 128, 128], P(None, 'mem', 'lev'), may hold values from -6 to 6
- perturb: bfloat16 [4096, 128, 5, 128], P('lev', 'mem'), may hold values from -6 to 6
- member_weights: float32 [128], P('mem'), may hold values from 0.25 to 4
- blocks: bfloat16 [64, 16, 64, 64], P(None, 'mem'), may hold values from -0.1875 to 0.1875
- block_cols: int32 [64, 16], replicated, may hold values from 0 to 63, as said below
- vertical: float32 [128, 128], replicated, may hold values from -4 to 4
Outputs:
- increment: float32 [4096, 5, 128], P(('lev', 'mem'))
Inputs may be any that keep to these rules, and one draw needn't show every extreme that they name: Within a block row the 16 block columns are distinct, and for every j the column block_cols[:, j] names each of the 64 block rows exactly once.
All inputs are finite; a program needn't handle non-finite values.
Results may differ from a plain program's by a relative error of at most 0.0003.
Values may be sent and summed in bfloat16 or wider, within the bound.
No kernel may reach another device: no remote copies, remote signals or barrier semaphores. Data moves between devices by JAX's collectives and lax.ppermute only.
A program may use at most 192 MiB of HBM per device.

v0:
```python
import math
import jax
import jax.numpy as jnp
from jax import lax
from jax.sharding import PartitionSpec as P


def shards(control, perturb, member_weights, blocks, block_cols, vertical):
    nodes_all, mem_dev, lev_dev = control.shape
    num_blocks, stored_count = block_cols.shape
    block_size = nodes_all // num_blocks
    columns = mem_dev * lev_dev
    source = control.reshape(num_blocks, block_size, columns)
    row_numbers = jnp.broadcast_to(
        jnp.arange(num_blocks, dtype=jnp.int32)[:, None], block_cols.shape
    )
    stored_numbers = jnp.arange(stored_count, dtype=jnp.int32)[None, :]
    inverse = jnp.zeros_like(block_cols).at[block_cols, stored_numbers].set(row_numbers)
    empty = jnp.zeros((num_blocks, block_size, columns), jnp.float32)
    summed = empty
    shard_piece = lax.all_gather(blocks, "mem", axis=1, tiled=True)
    count = shard_piece.shape[1]
    for offset in range(count):
        chosen = lax.dynamic_index_in_dim(block_cols, offset, 1, keepdims=False)
        picked = jnp.take(source, chosen, axis=0)
        tile_set = shard_piece[:, offset].astype(jnp.float32)
        summed = summed + jnp.einsum(
            "ipq,iqc->ipc", tile_set, picked, precision=lax.Precision.HIGHEST
        )
    horizontal = summed
    summed = empty
    shard_piece = lax.all_gather(blocks, "mem", axis=1, tiled=True)
    count = shard_piece.shape[1]
    for offset in range(count):
        owners = lax.dynamic_index_in_dim(inverse, offset, 1, keepdims=False)
        tile_set = shard_piece[:, offset].astype(jnp.float32)
        product = jnp.einsum("ipq,ipc->iqc", tile_set, horizontal, precision=lax.Precision.HIGHEST)
        summed = summed + jnp.take(product, owners, axis=0)
    level_groups = lax.axis_size("lev")
    arranged = summed.reshape(1, nodes_all, columns)
    transposed = lax.all_to_all(arranged, "lev", split_axis=1, concat_axis=0, tiled=True)
    owned_nodes = transposed.shape[1]
    split_levels = transposed.reshape(level_groups, owned_nodes, mem_dev, lev_dev)
    vertical_split = vertical.reshape(vertical.shape[0], level_groups, lev_dev)
    vertical_applied = jnp.einsum(
        "snkm,lsm->nkl", split_levels, vertical_split, precision=lax.Precision.HIGHEST
    )
    members_all = mem_dev * lax.axis_size("mem")
    weighted = vertical_applied * (member_weights / math.sqrt(members_all - 1))[None, :, None]
    return lax.psum_scatter(
        jnp.sum(perturb.astype(jnp.float32) * weighted[:, :, None, :], axis=1),
        "mem",
        scatter_dimension=0,
        tiled=True,
    )


def solution(mesh):
    in_specs = (
        P(None, "mem", "lev"),
        P("lev", "mem", None, None),
        P("mem"),
        P(None, "mem", None, None),
        P(),
        P(),
    )
    out_specs = P(("lev", "mem"), None, None)
    return jax.shard_map(shards, mesh=mesh, in_specs=in_specs, out_specs=out_specs, check_vma=False)
```

profile of v0, /device:TPU:0, one launch (start us, length us, event | category | flops | bytes accessed | tf_op | source)
XLA Modules:
  0.0 441.6 jit_solution(11678037962666474546)
XLA Ops:
  7.3 4.6 %reshape.26 = f32[64,64,128]{1,0,2:T(8,128)} reshape(f32[4096,8,16]{0,2,1:T(8,128)} %param.8) | data formatting | bytes 4194304 | tf_op jit(solution)/shard_map/reshape | solution.py:13
  11.9 3.8 copy.64
  15.8 2.1 gather_fusion.10
  31.9 2.1 gather_fusion.3
  40.1 2.1 gather_fusion.12
  42.2 2.1 gather_fusion.11
  48.7 4.8 %scatter_custom_fusion = s32[1024]{0:T(1024)S(1)} fusion(s32[1024]{0:T(1024)S(1)} %reshape.290, s32[1024]{0:T(1024)S(1)} %reshape.292, s32[]{:T(128)} %constant.116.clone.1), kind=kCustom, calls=%fused_computation.219 | custom fusion | bytes 4100
  53.7 68.5 %all-gather.2.cloned.1.call-done = bf16[64,16,64,64]{3,2,0,1:T(8,128)(2,1)} async-done(((bf16[64,1,64,64]{3,2,0,1:T(8,128)(2,1)}), bf16[64,16,64,64]{3,2,0,1:T(8,128)(2,1)}) %all-gather.2.cloned.1.call-update) | async-done | bytes 8388624 | tf_op jit(solution)/shard_map/all_gather | solution.py:32
  122.2 3.3 fusion.10
  125.5 3.3 fusion.12
  128.8 3.2 fusion.14
  132.0 4.7 %fusion.16 = f32[64,128,64]{1,2,0:T(8,128)} fusion(f32[64,64,128]{2,1,0:T(8,128)} %gather_fusion.7, pred[64]{0:T(512)(128)(4,1)S(1)} %get-tuple-element.114, bf16[64,16,64,64]{3,2,0,1:T(8,128)(2,1)} %all-gather.2.cloned.1.call-done), kind=kOutput, calls=%fused_computation.66 | convolution fusion | flops 403177472 | bytes 5242944 | tf_op jit(solution)/shard_map/ipq,iqc->ipc/dot_general | solution.py:27
  136.7 2.6 fusion.18
  139.4 2.6 fusion.2
  142.0 2.6 fusion.20
  144.6 2.7 fusion.22
  147.3 2.9 fusion.24
  150.2 2.7 fusion.26
  152.8 2.6 fusion.28
  155.5 2.7 fusion.4
  158.2 2.7 fusion.6
  160.9 2.7 fusion.8
  163.6 2.6 fusion
  166.2 11.1 %add_add_fusion = f32[64,128,64]{1,2,0:T(8,128)S(1)} fusion(f32[64,128,64]{1,2,0:T(8,128)} %fusion, f32[64,128,64]{1,2,0:T(8,128)} %fusion.2, f32[64,128,64]{1,2,0:T(8,128)} %fusion.4, f32[64,128,64]{1,2,0:T(8,128)} %fusion.6, f32[64,128,64]{1,2,0:T(8,128)} %fusion.8, f32[64,128,64]{1,2,0:T(8,128)S(1)} %fusion.10, f32[64,128,64]{1,2,0:T(8,128)S(1)} %fusion.12, ...), kind=kOutput, calls=%fused_computation.82 | convolution fusion | flops 411041792 | bytes 36700224 | tf_op jit(solution)/shard_map/ipq,iqc->ipc/dot_general | solution.py:27
  177.4 4.2 convolution_bitcast_fusion.15
  181.6 3.6 gather_fusion.16
  185.2 4.0 convolution_bitcast_fusion.14
  189.1 3.6 gather_fusion.17
  192.8 4.0 convolution_bitcast_fusion.13
  196.8 3.7 gather_fusion.18
  200.4 4.0 convolution_bitcast_fusion.12
  204.4 3.7 gather_fusion.19
  208.1 4.0 convolution_bitcast_fusion.11
  212.0 3.6 gather_fusion.20
  215.7 3.9 convolution_bitcast_fusion.10
  219.6 3.6 gather_fusion.21
  223.2 3.9 convolution_bitcast_fusion.9
  227.2 3.6 gather_fusion.22
  230.7 3.9 convolution_bitcast_fusion.8
  234.7 3.6 gather_fusion.23
  238.2 4.4 convolution_bitcast_fusion.7
  242.6 3.6 gather_fusion.24
  246.2 3.9 convolution_bitcast_fusion.6
  250.1 3.6 gather_fusion.25
  253.7 4.0 convolution_bitcast_fusion.5
  257.7 3.6 gather_fusion.26
  261.3 3.9 convolution_bitcast_fusion.4
  265.2 3.6 gather_fusion.27
  268.9 3.9 convolution_bitcast_fusion.3
  272.8 3.6 gather_fusion.28
  276.4 3.9 convolution_bitcast_fusion.2
  280.3 3.6 gather_fusion.29
  283.9 4.0 convolution_bitcast_fusion.1
  287.9 3.6 gather_fusion.30
  291.5 4.2 convolution_bitcast_fusion
  295.7 3.8 gather_fusion.31
  299.4 12.2 %select_add_fusion = f32[64,64,128]{2,1,0:T(8,128)} fusion(f32[64,64,128]{2,1,0:T(8,128)} %gather_fusion.31, f32[64,64,128]{2,1,0:T(8,128)} %gather_fusion.30, f32[64,64,128]{2,1,0:T(8,128)} %gather_fusion.29, f32[64,64,128]{2,1,0:T(8,128)} %gather_fusion.28, f32[64,64,128]{2,1,0:T(8,128)} %gather_fusion.27, f32[64,64,128]{2,1,0:T(8,128)} %gather_fusion.26, ...), kind=kLoop, calls=%fused_computation.35 | loop fusion | flops 16252928 | bytes 35652608 | tf_op jit(solution)/shard_map/add | solution.py:38
  311.7 4.5 %all-to-all-start = ((f32[1,4096,128]{2,0,1:T(1,128)}), f32[1,4096,128]{2,0,1:T(1,128)S(1)}, u32[]{:S(2)}, u32[]{:S(2)}) async-start(f32[1,4096,128]{2,0,1:T(1,128)} %bitcast.263), calls=%async_computation | async-start | bytes 4194304 | tf_op jit(solution)/shard_map/all_to_all | solution.py:41
  316.4 31.7 %all-to-all-done = f32[1,4096,128]{2,0,1:T(1,128)S(1)} async-done(((f32[1,4096,128]{2,0,1:T(1,128)}), f32[1,4096,128]{2,0,1:T(1,128)S(1)}, u32[]{:S(2)}, u32[]{:S(2)}) %all-to-all-start) | async-done | bytes 2097184 | tf_op jit(solution)/shard_map/all_to_all | solution.py:41
  348.0 4.1 copy.98
  352.1 3.4 copy.120
  355.5 3.6 bitcast_multiply_fusion
  360.4 5.6 %multiply_reduce_fusion = f32[512,5,128]{2,1,0:T(8,128)} fusion(bf16[512,8,5,128]{3,1,2,0:T(8,128)(2,1)S(1)} %bitcast.266, f32[512,8,128]{2,1,0:T(8,128)S(1)} %copy.101), kind=kLoop, calls=%fused_computation.33 | loop fusion | flops 7536640 | bytes 8650752 | tf_op jit(solution)/shard_map/reduce_sum | solution.py:51
  366.0 67.1 %reduce-scatter.2.cloned.1.call-done = f32[32,5,128]{2,1,0:T(8,128)} async-done(((f32[512,5,128]{2,1,0:T(8,128)}), f32[32,5,128]{2,1,0:T(8,128)}) %reduce-scatter.2.cloned.1.call-update) | async-done | bytes 81936 | tf_op jit(solution)/shard_map/reduce_scatter | solution.py:50
  (93 shorter events, 28.6 us)
Async XLA Ops:
  6.5 115.6 %all-gather.2.cloned.1.call-start = ((), (), s32[]{:S(2)}) async-start(), calls=%async_computation.2 | async-start | bytes 17825792 | tf_op jit(solution)/shard_map/all_gather | solution.py:32
  11.9 3.8 copy-start.16
  46.2 2.0 copy-start.17
  46.2 2.1 copy-start.18
  53.6 71.9 %copy-start.3 = (f32[64,64,128]{2,1,0:T(8,128)S(1)}, f32[64,64,128]{2,1,0:T(8,128)}, u32[]{:S(2)}) copy-start(f32[64,64,128]{2,1,0:T(8,128)} %gather_fusion.9) | copy-start | bytes 6291460
  122.2 14.5 %copy-start = (bf16[64,16,64,64]{3,2,0,1:T(8,128)(2,1)S(1)}, bf16[64,16,64,64]{3,2,0,1:T(8,128)(2,1)}, u32[]{:S(2)}) copy-start(bf16[64,16,64,64]{3,2,0,1:T(8,128)(2,1)} %all-gather.2.cloned.1.call-done) | copy-start | bytes 25165828
  132.0 4.7 %copy-start.4 = (f32[64,64,128]{2,1,0:T(8,128)S(1)}, f32[64,64,128]{2,1,0:T(8,128)}, u32[]{:S(2)}) copy-start(f32[64,64,128]{2,1,0:T(8,128)} %gather_fusion.6) | copy-start | bytes 6291460
  136.7 2.6 copy-start.5
  139.3 2.6 copy-start.6
  142.0 2.6 copy-start.7
  144.6 2.7 copy-start.8
  147.3 2.9 copy-start.9
  150.2 2.7 copy-start.10
  152.8 2.7 copy-start.11
  155.5 2.7 copy-start.12
  158.2 2.7 copy-start.13
  160.9 2.7 copy-start.14
  163.6 2.6 copy-start.1
  295.7 3.8 copy-start.2
  311.7 4.6 %copy-start.15 = (f32[128,128]{1,0:T(8,128)S(1)}, f32[128,128]{1,0:T(8,128)}, u32[]{:S(2)}) copy-start(f32[128,128]{1,0:T(8,128)} %param.13) | copy-start | bytes 196612
  311.7 4.6 %copy-start.19 = (f32[8]{0:T(128)S(1)}, f32[8]{0:T(128)}, u32[]{:S(2)}) copy-start(f32[8]{0:T(128)} %param.10) | copy-start | bytes 100
  311.7 36.3 %all-to-all-start = ((f32[1,4096,128]{2,0,1:T(1,128)}), f32[1,4096,128]{2,0,1:T(1,128)S(1)}, u32[]{:S(2)}, u32[]{:S(2)}) async-start(f32[1,4096,128]{2,0,1:T(1,128)} %bitcast.263), calls=%async_computation | async-start | bytes 4194304 | tf_op jit(solution)/shard_map/all_to_all | solution.py:41
  316.2 116.9 %reduce-scatter.2.cloned.1.call-start = ((), (), s32[]{:S(2)}) async-start(), calls=%async_computation.3 | async-start | bytes 2228224 | tf_op jit(solution)/shard_map/reduce_scatter | solution.py:50
  352.1 8.2 %slice-start = ((s8[5242880]{0:T(1024)(128)(4,1)}), s8[4194304]{0:T(1024)(128)(4,1)S(1)}, s32[]{:S(2)}) async-start(s8[5242880]{0:T(1024)(128)(4,1)} %bitcast.265), calls=%async_computation.4 | async-start | bytes 8388608
  355.5 4.9 %slice-start.1 = ((s8[5242880]{0:T(1024)(128)(4,1)}), s8[1048576]{0:T(1024)(128)(4,1)S(1)}, s32[]{:S(2)}) async-start(s8[5242880]{0:T(1024)(128)(4,1)} %bitcast.265), calls=%async_computation.5 | async-start | bytes 2097152
Sparse Core Ops, SparseCore 0:
  9.8 112.3 all-gather.1
  366.1 66.8 reduce-scatter.1
where the time goes:
time: 448 us; the launch traced here: 442 us
  waiting for transfers between devices  168 us (38%)
  matrix products  123 us (27%)
  local copies, waits for them, and re-layouts  114 us (25%)
  other arithmetic  18.2 us (4%)
  between operations  13.9 us (3%)
  starting transfers between devices  4.52 us (1%)
    all_gather x1, waiting for transfers between devices, shards(): shard_piece = lax.all_gather(blocks, 'mem', axis=1, tiled=True)  68.5 us
    reduce_scatter x1, waiting for transfers between devices, shards(): lax.psum_scatter(jnp.sum(perturb.astype(jnp.float32) * weighted[:, :, Non...  67.1 us
    dot_general x16, matrix products, shards(): jnp.einsum('ipq,ipc->iqc', tile_set, horizontal, precision=lax.Precision....  64.1 us
    gather x16, local copies, waits for them, and re-layouts, shards(): summed = summed + jnp.take(product, owners, axis=0)  58 us
    dot_general x16, matrix products, shards(): jnp.einsum('ipq,iqc->ipc', tile_set, picked, precision=lax.Precision.HIGH...  55.1 us
    gather x16, local copies, waits for them, and re-layouts, shards(): picked = jnp.take(source, chosen, axis=0)  32.4 us
    all_to_all x1, waiting for transfers between devices, shards(): lax.all_to_all(arranged, 'lev', split_axis=1, concat_axis=0, tiled=True)  31.7 us
    add x1, other arithmetic, shards(): summed = summed + jnp.take(product, owners, axis=0)  12.2 us
  transfers between devices with their start and end apart: 3, of which 3 were waited for; matrix products, arithmetic and copies ran while one was open for 11% of the time, Pallas kernels for 0%

commit v1 on v0

--- a/solution.py
+++ b/solution.py
@@ -29,7 +29,9 @@
         )
     horizontal = summed
     summed = empty
-    shard_piece = lax.all_gather(blocks, "mem", axis=1, tiled=True)
+    shard_piece = jnp.concatenate(
+        lax.all_to_all(jnp.stack([blocks] * lax.axis_size("mem")), "mem", 0, 0), axis=1
+    )
     count = shard_piece.shape[1]
     for offset in range(count):
         owners = lax.dynamic_index_in_dim(inverse, offset, 1, keepdims=False)

time: 448 us -> 514 us (1.15)
  local copies, waits for them, and re-layouts: 114 us -> 173 us
  matrix products: 123 us -> 106 us
  waiting for transfers between devices: 168 us -> 181 us
  starting transfers between devices: 4.52 us -> 13.2 us
    all_to_all x0 -> x1, waiting for transfers between devices: none -> 75.9 us  [shards(): lax.all_to_all(jnp.stack([blocks] * lax.axis_size('mem')), 'mem', 0, 0)]
    all_gather x1, waiting for transfers between devices: 68.5 us -> 4.44 us  [shards(): shard_piece = lax.all_gather(blocks, 'mem', axis=1, tiled=True)]
    unnamed x50 -> x61, local copies, waits for them, and re-layouts: 8.57 us -> 53.3 us
    dot_general x16, matrix products: 64.1 us -> 48.8 us  [shards(): jnp.einsum('ipq,ipc->iqc', tile_set, horizontal, precision=lax.Precision....]
    reshape x0 -> x1, local copies, waits for them, and re-layouts: none -> 15 us  [shards(): jnp.concatenate(lax.all_to_all(jnp.stack([blocks] * lax.axis_size('mem'))...]
    all_to_all x0 -> x1, starting transfers between devices: none -> 8.34 us  [shards(): lax.all_to_all(jnp.stack([blocks] * lax.axis_size('mem')), 'mem', 0, 0)]
  transfers between devices with their start and end apart: 3 -> 4, of which waited for: 3 -> 4; matrix products, arithmetic and copies ran while one was open for 11% -> 21% of each run, Pallas kernels for 0% -> 0%
where the time goes in v1:
time: 514 us; the launch traced here: 506 us
  waiting for transfers between devices  181 us (35%)
  local copies, waits for them, and re-layouts  173 us (34%)
  matrix products  106 us (21%)
  other arithmetic  18.4 us (4%)
  between operations  14.2 us (3%)
  starting transfers between devices  13.2 us (3%)
    all_to_all x1, waiting for transfers between devices, shards(): lax.all_to_all(jnp.stack([blocks] * lax.axis_size('mem')), 'mem', 0, 0)  75.9 us
    reduce_scatter x1, waiting for transfers between devices, shards(): lax.psum_scatter(jnp.sum(perturb.astype(jnp.float32) * weighted[:, :, Non...  68.3 us
    gather x16, local copies, waits for them, and re-layouts, shards(): summed = summed + jnp.take(product, owners, axis=0)  56.5 us
    dot_general x16, matrix products, shards(): jnp.einsum('ipq,iqc->ipc', tile_set, picked, precision=lax.Precision.HIGH...  53.5 us
    unnamed x61, local copies, waits for them, and re-layouts  53.3 us
    dot_general x16, matrix products, shards(): jnp.einsum('ipq,ipc->iqc', tile_set, horizontal, precision=lax.Precision....  48.8 us
    gather x16, local copies, waits for them, and re-layouts, shards(): picked = jnp.take(source, chosen, axis=0)  32.6 us
    all_to_all x1, waiting for transfers between devices, shards(): lax.all_to_all(arranged, 'lev', split_axis=1, concat_axis=0, tiled=True)  31.7 us
  transfers between devices with their start and end apart: 4, of which 4 were waited for; matrix products, arithmetic and copies ran while one was open for 21% of the time, Pallas kernels for 0%

profile of v1, /device:TPU:0, one launch (start us, length us, event | category | flops | bytes accessed | tf_op | source)
XLA Modules:
  0.0 505.9 jit_solution(17651089940313222050)
XLA Ops:
  8.9 6.3 %broadcast_bitcast_fusion = bf16[16,1,64,64,64]{4,3,2,1,0:T(8,128)(2,1)} fusion(bf16[64,64,64]{1,2,0:T(8,128)(2,1)S(1)} %copy.51), kind=kLoop, calls=%fused_computation.303 | loop fusion | bytes 8912896
  15.2 19.8 %reshape.407 = bf16[16,2,131072]{2,1,0:T(2,128)(2,1)} reshape(bf16[16,1,64,64,64]{4,3,2,1,0:T(8,128)(2,1)} %broadcast_bitcast_fusion) | data formatting | bytes 16777216
  35.0 8.3 %all-to-all-start = ((bf16[16,2,131072]{2,1,0:T(2,128)(2,1)}), bf16[16,2,131072]{2,1,0:T(2,128)(2,1)}, u32[]{:S(2)}, u32[]{:S(2)}) async-start(bf16[16,2,131072]{2,1,0:T(2,128)(2,1)} %reshape.407), calls=%async_computation | async-start | bytes 16777216 | tf_op jit(solution)/shard_map/all_to_all | solution.py:33
  43.3 3.1 reshape.35
  46.4 3.8 copy.34
  83.4 4.3 scatter_custom_fusion
  87.9 75.9 %all-to-all-done = bf16[16,2,131072]{2,1,0:T(2,128)(2,1)} async-done(((bf16[16,2,131072]{2,1,0:T(2,128)(2,1)}), bf16[16,2,131072]{2,1,0:T(2,128)(2,1)}, u32[]{:S(2)}, u32[]{:S(2)}) %all-to-all-start) | async-done | bytes 8388640 | tf_op jit(solution)/shard_map/all_to_all | solution.py:33
  163.8 19.3 %reshape.408 = bf16[16,1,64,64,64]{4,3,2,1,0:T(8,128)(2,1)} reshape(bf16[16,2,131072]{2,1,0:T(2,128)(2,1)} %all-to-all-done) | data formatting | bytes 16777216
  183.1 15.0 %bitcast_bitcast_fusion = bf16[64,16,64,64]{2,3,0,1:T(8,128)(2,1)} fusion(bf16[16,1,64,64,64]{4,3,2,1,0:T(8,128)(2,1)} %reshape.408), kind=kLoop, calls=%fused_computation.302 | loop fusion | bytes 16777216 | tf_op jit(solution)/shard_map/reshape | solution.py:32
  198.1 4.4 all-gather.2.cloned.1.call-done
  202.5 2.7 fusion.10
  205.2 3.9 fusion.12
  209.2 3.2 fusion.14
  212.4 3.3 fusion.16
  215.7 2.7 fusion.18
  218.4 2.7 fusion.2
  221.1 2.6 fusion.20
  223.8 2.7 fusion.22
  226.4 3.1 fusion.24
  229.5 2.7 fusion.26
  232.2 2.7 fusion.28
  234.9 2.7 fusion.4
  237.6 2.7 fusion.6
  240.3 2.6 fusion.8
  242.9 2.7 fusion
  245.6 10.6 %add_add_fusion = f32[64,128,64]{1,2,0:T(8,128)S(1)} fusion(f32[64,128,64]{1,2,0:T(8,128)} %fusion, f32[64,128,64]{1,2,0:T(8,128)} %fusion.2, f32[64,128,64]{1,2,0:T(8,128)} %fusion.4, f32[64,128,64]{1,2,0:T(8,128)} %fusion.6, f32[64,128,64]{1,2,0:T(8,128)} %fusion.8, f32[64,128,64]{1,2,0:T(8,128)S(1)} %fusion.10, f32[64,128,64]{1,2,0:T(8,128)S(1)} %fusion.12, ...), kind=kOutput, calls=%fused_computation.82 | convolution fusion | flops 411041792 | bytes 36700224 | tf_op jit(solution)/shard_map/ipq,iqc->ipc/dot_general | solution.py:27
  256.1 4.1 convolution_bitcast_fusion.15
  260.2 3.9 convolution_bitcast_fusion.14
  264.2 3.7 convolution_bitcast_fusion.13
  267.9 3.8 convolution_bitcast_fusion.12
  271.7 3.9 convolution_bitcast_fusion.11
  275.6 3.7 convolution_bitcast_fusion.10
  279.4 2.5 convolution_bitcast_fusion.9
  284.4 2.5 convolution_bitcast_fusion.7
  286.9 2.6 convolution_bitcast_fusion.6
  289.5 2.8 convolution_bitcast_fusion.5
  292.3 2.5 convolution_bitcast_fusion.4
  294.8 2.5 convolution_bitcast_fusion.3
  297.3 2.6 convolution_bitcast_fusion.2
  299.9 2.6 convolution_bitcast_fusion.1
  302.4 2.5 convolution_bitcast_fusion
  307.2 3.6 gather_fusion.17
  310.8 3.6 gather_fusion.18
  314.5 3.6 gather_fusion.19
  318.1 3.6 gather_fusion.20
  321.6 3.6 gather_fusion.21
  325.2 3.6 gather_fusion.22
  328.9 3.6 gather_fusion.23
  332.5 3.6 gather_fusion.24
  336.0 3.6 gather_fusion.25
  339.7 3.7 gather_fusion.26
  343.3 3.7 gather_fusion.27
  347.0 3.6 gather_fusion.28
  350.6 3.6 gather_fusion.29
  354.2 3.7 gather_fusion.30
  357.8 3.7 gather_fusion.31
  361.5 12.3 %select_add_fusion = f32[64,64,128]{2,1,0:T(8,128)} fusion(f32[64,64,128]{2,1,0:T(8,128)} %gather_fusion.31, f32[64,64,128]{2,1,0:T(8,128)} %gather_fusion.30, f32[64,64,128]{2,1,0:T(8,128)} %gather_fusion.29, f32[64,64,128]{2,1,0:T(8,128)} %gather_fusion.28, f32[64,64,128]{2,1,0:T(8,128)} %gather_fusion.27, f32[64,64,128]{2,1,0:T(8,128)} %gather_fusion.26, ...), kind=kLoop, calls=%fused_computation.35 | loop fusion | flops 16252928 | bytes 35652608 | tf_op jit(solution)/shard_map/add | solution.py:40
  373.8 4.8 all-to-all-start.1
  378.7 31.7 %all-to-all-done.1 = f32[1,4096,128]{2,0,1:T(1,128)S(1)} async-done(((f32[1,4096,128]{2,0,1:T(1,128)}), f32[1,4096,128]{2,0,1:T(1,128)S(1)}, u32[]{:S(2)}, u32[]{:S(2)}) %all-to-all-start.1) | async-done | bytes 2097184 | tf_op jit(solution)/shard_map/all_to_all | solution.py:43
  410.4 4.3 copy.54
  414.7 3.2 copy.60
  418.0 3.7 bitcast_multiply_fusion
  422.9 5.8 %multiply_reduce_fusion = f32[512,5,128]{2,1,0:T(8,128)} fusion(bf16[512,8,5,128]{3,1,2,0:T(8,128)(2,1)S(1)} %bitcast.311, f32[512,8,128]{2,1,0:T(8,128)S(1)} %copy.57), kind=kLoop, calls=%fused_computation.33 | loop fusion | flops 7536640 | bytes 8650752 | tf_op jit(solution)/shard_map/reduce_sum | solution.py:53
  428.8 68.3 %reduce-scatter.2.cloned.1.call-done = f32[32,5,128]{2,1,0:T(8,128)} async-done(((f32[512,5,128]{2,1,0:T(8,128)}), f32[32,5,128]{2,1,0:T(8,128)}) %reduce-scatter.2.cloned.1.call-update) | async-done | bytes 81936 | tf_op jit(solution)/shard_map/reduce_scatter | solution.py:52
  (109 shorter events, 43.3 us)
Async XLA Ops:
  6.5 196.0 %all-gather.2.cloned.1.call-start = ((), (), s32[]{:S(2)}) async-start(), calls=%async_computation.3 | async-start | bytes 17825792 | tf_op jit(solution)/shard_map/all_gather | solution.py:21
  35.0 8.4 %copy-start.14 = (f32[4096,8,16]{0,2,1:T(8,128)S(1)}, f32[4096,8,16]{0,2,1:T(8,128)}, u32[]{:S(2)}) copy-start(f32[4096,8,16]{0,2,1:T(8,128)} %param.8) | copy-start | bytes 6291460
  35.0 128.8 %all-to-all-start = ((bf16[16,2,131072]{2,1,0:T(2,128)(2,1)}), bf16[16,2,131072]{2,1,0:T(2,128)(2,1)}, u32[]{:S(2)}, u32[]{:S(2)}) async-start(bf16[16,2,131072]{2,1,0:T(2,128)(2,1)} %reshape.407), calls=%async_computation | async-start | bytes 16777216 | tf_op jit(solution)/shard_map/all_to_all | solution.py:33
  46.4 3.8 copy-start.16
  80.9 2.0 copy-start.17
  80.9 2.1 copy-start.18
  183.1 19.5 %copy-start.2 = (f32[64,64,128]{2,1,0:T(8,128)S(1)}, f32[64,64,128]{2,1,0:T(8,128)}, u32[]{:S(2)}) copy-start(f32[64,64,128]{2,1,0:T(8,128)} %gather_fusion.10) | copy-start | bytes 6291460
  202.5 13.2 %copy-start = (bf16[64,16,64,64]{3,2,0,1:T(8,128)(2,1)S(1)}, bf16[64,16,64,64]{3,2,0,1:T(8,128)(2,1)}, u32[]{:S(2)}) copy-start(bf16[64,16,64,64]{3,2,0,1:T(8,128)(2,1)} %all-gather.2.cloned.1.call-done) | copy-start | bytes 25165828
  212.4 3.4 copy-start.3
  215.7 2.7 copy-start.4
  218.4 2.7 copy-start.5
  221.1 2.7 copy-start.6
  223.8 2.7 copy-start.7
  226.4 3.1 copy-start.8
  229.5 2.7 copy-start.9
  232.2 2.7 copy-start.10
  234.9 2.7 copy-start.11
  237.6 2.7 copy-start.12
  240.3 2.6 copy-start.13
  242.9 2.7 copy-start.1
  256.1 23.2 %slice-start = ((s8[16777216]{0:T(1024)(128)(4,1)}), s8[4194304]{0:T(1024)(128)(4,1)S(1)}, s32[]{:S(2)}) async-start(s8[16777216]{0:T(1024)(128)(4,1)} %bitcast.306), calls=%async_computation.5 | async-start | bytes 8388608
  260.2 19.1 %slice-start.1 = ((s8[16777216]{0:T(1024)(128)(4,1)}), s8[4194304]{0:T(1024)(128)(4,1)S(1)}, s32[]{:S(2)}) async-start(s8[16777216]{0:T(1024)(128)(4,1)} %bitcast.306), calls=%async_computation.6 | async-start | bytes 8388608
  267.9 11.5 %slice-start.2 = ((s8[16777216]{0:T(1024)(128)(4,1)}), s8[4194304]{0:T(1024)(128)(4,1)S(1)}, s32[]{:S(2)}) async-start(s8[16777216]{0:T(1024)(128)(4,1)} %bitcast.306), calls=%async_computation.7 | async-start | bytes 8388608
  271.7 7.7 %slice-start.3 = ((s8[16777216]{0:T(1024)(128)(4,1)}), s8[4194304]{0:T(1024)(128)(4,1)S(1)}, s32[]{:S(2)}) async-start(s8[16777216]{0:T(1024)(128)(4,1)} %bitcast.306), calls=%async_computation.8 | async-start | bytes 8388608
  373.8 4.9 copy-start.15
  373.8 5.0 copy-start.19
  373.8 36.6 %all-to-all-start.1 = ((f32[1,4096,128]{2,0,1:T(1,128)}), f32[1,4096,128]{2,0,1:T(1,128)S(1)}, u32[]{:S(2)}, u32[]{:S(2)}) async-start(f32[1,4096,128]{2,0,1:T(1,128)} %bitcast.308), calls=%async_computation.1 | async-start | bytes 4194304 | tf_op jit(solution)/shard_map/all_to_all | solution.py:43
  378.6 118.5 %reduce-scatter.2.cloned.1.call-start = ((), (), s32[]{:S(2)}) async-start(), calls=%async_computation.4 | async-start | bytes 2228224 | tf_op jit(solution)/shard_map/reduce_scatter | solution.py:52
  410.4 12.5 %slice-start.4 = ((s8[5242880]{0:T(1024)(128)(4,1)}), s8[1048576]{0:T(1024)(128)(4,1)S(1)}, s32[]{:S(2)}) async-start(s8[5242880]{0:T(1024)(128)(4,1)} %bitcast.310), calls=%async_computation.9 | async-start | bytes 2097152
  418.0 4.9 slice-start.5
Sparse Core Ops, SparseCore 0:
  9.8 192.7 all-gather.1
  428.9 68.0 reduce-scatter.1
